TPU v7x, 32 devices: a whole 2x2x4 slice. The times are simulated.
32 devices in a mesh: grid: 8 (over y, x, core), ao: 4 (over z).
Axes of the slice: x: 2, y: 2, z: 4, core: 2. Of those that a mesh axis runs over, the one named last changes fastest.
Arguments:
- trial: bfloat16 [12288, 16, 2, 128], P('ao'), may hold values from -0.15625 to 0.15625
- occupied: bfloat16 [12288, 2, 128], P('ao'), may hold values from -0.15625 to 0.15625
- colloc: bfloat16 [32, 128, 1536], P('grid'), may hold values from -3 to 3
- blocks: int32 [32, 12], P('grid'), may hold values from 0 to 95, as said below
- coords: float32 [32, 3, 128], P('grid'), may hold values from 0 to 4
- weights: float32 [32, 128], P('grid'), may hold values from 0.02 to 0.2
Outputs:
- exchange: float32 [16, 12288, 2, 128], P('ao', 'grid')
Inputs may be any that keep to these rules, and one draw needn't show every extreme that they name: The 12 blocks of a batch are distinct and lie among 24 cyclically consecutive shell blocks.
All inputs are finite; a program needn't handle non-finite values.
Results may differ from a plain program's by a relative error of at most 0.0053.
Values may be sent and summed in bfloat16 or wider, within the bound.
No kernel may reach another device: no remote copies, remote signals or barrier semaphores. Data moves between devices by JAX's collectives and lax.ppermute only.
A program may use at most 192 MiB of HBM per device.

v0:
```python
import jax
import jax.numpy as jnp
from jax import lax
from jax.sharding import PartitionSpec as P

BLK = 128
NOCC = 128
P_SIZE = 128
SIG = 12


def kernel_matrix(points, quad):
    differ = points[:, :, None] - points[:, None, :]
    square = jnp.sum(differ * differ, axis=0)
    return quad[:, None] * quad[None, :] / jnp.sqrt(square + 0.25)


def pair_exchange(lg_half, og_half, kernel):
    lreal = lg_half[:, :, 0]
    limag = lg_half[:, :, 1]
    oreal = og_half[:, 0]
    oimag = og_half[:, 1]
    f32 = jnp.float32
    rho_real = jnp.einsum("gvi,hi->vgh", lreal, oreal, preferred_element_type=f32) + jnp.einsum(
        "gvi,hi->vgh", limag, oimag, preferred_element_type=f32
    )
    rho_imag = jnp.einsum("gvi,hi->vgh", limag, oreal, preferred_element_type=f32) - jnp.einsum(
        "gvi,hi->vgh", lreal, oimag, preferred_element_type=f32
    )
    m_real = (rho_real * kernel[None]).astype(jnp.bfloat16)
    m_imag = (rho_imag * kernel[None]).astype(jnp.bfloat16)
    e_real = jnp.einsum("vgh,hj->gvj", m_real, oreal, preferred_element_type=f32) - jnp.einsum(
        "vgh,hj->gvj", m_imag, oimag, preferred_element_type=f32
    )
    e_imag = jnp.einsum("vgh,hj->gvj", m_real, oimag, preferred_element_type=f32) + jnp.einsum(
        "vgh,hj->gvj", m_imag, oreal, preferred_element_type=f32
    )
    return jnp.stack([e_real, e_imag], axis=2).astype(jnp.bfloat16)


def project_back(values, potential):
    return lax.dot_general(
        values, potential, (((0,), (0,)), ((), ())), preferred_element_type=jnp.float32
    )


def on_device(trial, occupied, colloc, blocks, coords, weights):
    ao_index = lax.axis_index("ao")
    local_rows = trial.shape[0]
    nblk_local = local_rows // BLK
    nvec_all = trial.shape[1]
    width = nvec_all * 2 * NOCC
    nvec_mine = nvec_all // lax.axis_size("ao")
    nblk_total = nblk_local * lax.axis_size("ao")
    batches = colloc.shape[0]
    combined = jnp.concatenate(
        [trial.reshape(local_rows, width), occupied.reshape(local_rows, 2 * NOCC)], axis=1
    )
    combined = combined.reshape(nblk_local, BLK, width + 2 * NOCC)

    def density(batch_items):
        values, block_ids = batch_items
        local_ids = block_ids - ao_index * nblk_local
        inside = (local_ids >= 0) & (local_ids < nblk_local)
        picked = combined[jnp.clip(local_ids, 0, nblk_local - 1)] * inside[:, None, None].astype(
            jnp.bfloat16
        )
        return jnp.dot(
            values, picked.reshape(SIG * BLK, width + 2 * NOCC), preferred_element_type=jnp.float32
        )

    partial_dens = lax.map(density, (colloc, blocks))
    trial_part = partial_dens[:, :, :width].reshape(batches, P_SIZE, nvec_all, 2 * NOCC)
    trial_dens = lax.psum_scatter(trial_part, "ao", scatter_dimension=2, tiled=True)
    occ_dens = lax.psum(partial_dens[:, :, width:], "ao")
    lg_all = trial_dens.reshape(batches, P_SIZE, nvec_mine, 2, NOCC).astype(jnp.bfloat16)
    og_all = occ_dens.reshape(batches, P_SIZE, 2, NOCC).astype(jnp.bfloat16)

    def potential_of(batch_items):
        lg_half, og_half, points, quad = batch_items
        return pair_exchange(lg_half, og_half, kernel_matrix(points, quad)).reshape(
            P_SIZE, nvec_mine * 2 * NOCC
        )

    potentials = lax.map(potential_of, (lg_all, og_all, coords, weights))
    mine_width = nvec_mine * 2 * NOCC
    nown = nblk_total // lax.axis_size("grid")

    def add_batch(running, batch_items):
        values, block_ids, potential = batch_items
        contrib = project_back(values, potential).reshape(SIG, BLK, mine_width)
        return (running.at[block_ids].add(contrib), None)

    panel, _ = lax.scan(
        add_batch,
        jnp.zeros((nblk_total, BLK, mine_width), jnp.float32),
        (colloc, blocks, potentials),
    )
    owned_rows = lax.psum_scatter(panel, "grid", scatter_dimension=0, tiled=True)
    return owned_rows.reshape(nown * BLK, nvec_mine, 2, NOCC).transpose(1, 0, 2, 3)


def solution(mesh):
    in_specs = (
        P("ao", None, None, None),
        P("ao", None, None),
        P("grid", None, None),
        P("grid", None),
        P("grid", None, None),
        P("grid", None),
    )
    out_specs = P("ao", "grid", None, None)
    return jax.shard_map(
        on_device, mesh=mesh, in_specs=in_specs, out_specs=out_specs, check_vma=False
    )
```

profile of v0, /device:TPU:0, one launch (start us, length us, event | category | flops | bytes accessed | tf_op | source)
XLA Modules:
  0.0 923.5 jit_solution(17151690536669517443)
XLA Ops:
  10.3 40.9 %concatenate.8 = bf16[24,128,4096]{2,1,0:T(8,128)(2,1)} reshape(bf16[3072,16,2,128]{3,2,1,0:T(2,128)(2,1)} %param.12) | data formatting | bytes 50331648 | tf_op jit(solution)/shard_map/concatenate | solution.py:56
  51.2 19.0 %pad_maximum_fusion.1 = bf16[24,128,4352]{2,1,0:T(8,128)(2,1)} fusion(bf16[24,128,256]{2,1,0:T(8,128)(2,1)} %concatenate.9, bf16[24,128,4096]{2,1,0:T(8,128)(2,1)} %concatenate.8), kind=kLoop, calls=%fused_computation.56 | loop fusion | flops 53477376 | bytes 53477376 | tf_op jit(solution)/shard_map/concatenate | solution.py:56
  70.2 98.2 %while.32 = (s32[]{:T(128)}, f32[4,128,4352]{2,1,0:T(8,128)}, bf16[4,128,1536]{2,1,0:T(8,128)(2,1)S(1)}, s32[4,12]{1,0:T(4,128)S(1)}, s32[]{:T(128)}, /*index=5*/bf16[24,128,4352]{2,1,0:T(8,128)(2,1)}, s32[]{:T(128)}) while((s32[]{:T(128)}, f32[4,128,4352]{2,1,0:T(8,128)}, bf16[4,128,1536]{2,1,0:T(8,128)(2,1)S(1)}, s32[4,12]{1,0:T(4,128)S(1)}, ...), condition=%wide.region_1.2_spmd, body=%wide.region_0.1_spmd.sunk | while | flops 1717961856 | bytes 69473664 | solution.py:72
  70.3 14.6 %gather_fusion = bf16[12,128,4352]{2,1,0:T(8,128)(2,1)} fusion(bf16[24,128,4352]{2,1,0:T(8,128)(2,1)} %get-tuple-element.337, s32[1024]{0:T(1024)S(1)} %pad_clamp_fusion.2), kind=kCustom, calls=%fused_computation.clone.1 | custom fusion | bytes 26738736 | tf_op jit(solution)/shard_map/while/body/eval_jaxpr/gather | solution.py:65
  84.9 6.5 broadcast_multiply_fusion.2
  94.7 14.9 %gather_fusion = bf16[12,128,4352]{2,1,0:T(8,128)(2,1)} fusion(bf16[24,128,4352]{2,1,0:T(8,128)(2,1)} %get-tuple-element.337, s32[1024]{0:T(1024)S(1)} %pad_clamp_fusion.2), kind=kCustom, calls=%fused_computation.clone.1 | custom fusion | bytes 26738736 | tf_op jit(solution)/shard_map/while/body/eval_jaxpr/gather | solution.py:65
  109.5 6.5 broadcast_multiply_fusion.2
  119.4 14.8 %gather_fusion = bf16[12,128,4352]{2,1,0:T(8,128)(2,1)} fusion(bf16[24,128,4352]{2,1,0:T(8,128)(2,1)} %get-tuple-element.337, s32[1024]{0:T(1024)S(1)} %pad_clamp_fusion.2), kind=kCustom, calls=%fused_computation.clone.1 | custom fusion | bytes 26738736 | tf_op jit(solution)/shard_map/while/body/eval_jaxpr/gather | solution.py:65
  134.2 6.5 broadcast_multiply_fusion.2
  144.0 14.6 %gather_fusion = bf16[12,128,4352]{2,1,0:T(8,128)(2,1)} fusion(bf16[24,128,4352]{2,1,0:T(8,128)(2,1)} %get-tuple-element.337, s32[1024]{0:T(1024)S(1)} %pad_clamp_fusion.2), kind=kCustom, calls=%fused_computation.clone.1 | custom fusion | bytes 26738736 | tf_op jit(solution)/shard_map/while/body/eval_jaxpr/gather | solution.py:65
  168.4 7.6 slice.19
  176.0 9.3 %copy.60 = f32[4,128,4352]{1,2,0:T(8,128)} copy(f32[4,128,4352]{2,1,0:T(8,128)} %get-tuple-element.136) | data formatting | bytes 17825792 | tf_op jit(solution)/shard_map/while | solution.py:72
  185.3 9.0 copy.61
  195.6 304.2 %all-reduce.3 = (bf16[4,128,256]{1,2,0:T(8,128)(2,1)}, bf16[4,128,16,256]{1,3,2,0:T(8,128)(2,1)}) all-reduce(f32[4,128,256]{1,2,0:T(8,128)S(1)} %slice-done, f32[4,128,16,256]{1,3,2,0:T(8,128)} %bitcast.195), channel_id=1, replica_groups=mesh['grid'=8,'ao'=4] {'ao'}, use_global_device_ids=true, to_apply=%region_3.4 | all-reduce | flops 2228224 | bytes 13369344 | tf_op jit(solution)/shard_map/psum | solution.py:75
  501.1 21.4 %while.33 = (s32[]{:T(128)}, bf16[4,128,1024]{1,2,0:T(8,128)(2,1)}, bf16[4,128,2,128]{1,3,2,0:T(8,128)(2,1)}, bf16[4,128,4,2,128]{1,4,3,2,0:T(8,128)(2,1)S(1)}, ...) while((s32[]{:T(128)}, bf16[4,128,1024]{1,2,0:T(8,128)(2,1)}, bf16[4,128,2,128]{1,3,2,0:T(8,128)(2,1)}, ...), condition=%wide.region_6.7_spmd, body=%wide.region_4.6_spmd.sunk | while | flops 135184384 | bytes 7283817 | solution.py:85
  522.5 16.2 %broadcast_in_dim.15 = f32[96,128,1024]{2,1,0:T(8,128)} broadcast(f32[]{:T(128)} %constant.69.clone.1), dimensions={} | broadcast | bytes 50331652 | tf_op jit(solution)/shard_map/broadcast_in_dim | solution.py:96
  538.7 75.3 %while.34 = (s32[]{:T(128)}, f32[96,128,1024]{2,1,0:T(8,128)}, s32[4,12]{1,0:T(4,128)S(1)}, bf16[4,128,1536]{2,1,0:T(8,128)(2,1)S(1)}, bf16[4,128,1024]{1,2,0:T(8,128)(2,1)}, /*index=5*/s32[]{:T(128)}) while((s32[]{:T(128)}, f32[96,128,1024]{2,1,0:T(8,128)}, s32[4,12]{1,0:T(4,128)S(1)}, bf16[4,128,1536]{2,1,0:T(8,128)(2,1)S(1)}, ...), condition=%wide.region_9.10_spmd, body=%wide.region_7.9_spmd.sunk | while | flops 404226080 | bytes 27394280 | solution.py:94
  543.6 13.9 %scatter_fusion = f32[96,128,1024]{2,1,0:T(8,128)} fusion(f32[96,128,1024]{2,1,0:T(8,128)} %get-tuple-element.367, s32[12]{0:T(128)S(1)} %fusion.76, f32[12,128,1024]{2,1,0:T(8,128)} %fusion.77), kind=kCustom, calls=%fused_computation.1.clone.1 | custom fusion | flops 1572864 | bytes 18874416 | tf_op jit(solution)/shard_map/while/body/eval_jaxpr/scatter-add | solution.py:92
  562.4 14.0 %scatter_fusion = f32[96,128,1024]{2,1,0:T(8,128)} fusion(f32[96,128,1024]{2,1,0:T(8,128)} %get-tuple-element.367, s32[12]{0:T(128)S(1)} %fusion.76, f32[12,128,1024]{2,1,0:T(8,128)} %fusion.77), kind=kCustom, calls=%fused_computation.1.clone.1 | custom fusion | flops 1572864 | bytes 18874416 | tf_op jit(solution)/shard_map/while/body/eval_jaxpr/scatter-add | solution.py:92
  581.4 13.9 %scatter_fusion = f32[96,128,1024]{2,1,0:T(8,128)} fusion(f32[96,128,1024]{2,1,0:T(8,128)} %get-tuple-element.367, s32[12]{0:T(128)S(1)} %fusion.76, f32[12,128,1024]{2,1,0:T(8,128)} %fusion.77), kind=kCustom, calls=%fused_computation.1.clone.1 | custom fusion | flops 1572864 | bytes 18874416 | tf_op jit(solution)/shard_map/while/body/eval_jaxpr/scatter-add | solution.py:92
  600.2 13.8 %scatter_fusion = f32[96,128,1024]{2,1,0:T(8,128)} fusion(f32[96,128,1024]{2,1,0:T(8,128)} %get-tuple-element.367, s32[12]{0:T(128)S(1)} %fusion.76, f32[12,128,1024]{2,1,0:T(8,128)} %fusion.77), kind=kCustom, calls=%fused_computation.1.clone.1 | custom fusion | flops 1572864 | bytes 18874416 | tf_op jit(solution)/shard_map/while/body/eval_jaxpr/scatter-add | solution.py:92
  614.1 285.8 %reduce-scatter.5.cloned.1.call-done = f32[12,128,1024]{2,1,0:T(8,128)} async-done(((f32[96,128,1024]{2,1,0:T(8,128)}), f32[12,128,1024]{2,1,0:T(8,128)}) %reduce-scatter.5.cloned.1.call-update) | async-done | bytes 6291472 | tf_op jit(solution)/shard_map/reduce_scatter | solution.py:99
  899.8 9.2 reshape.186
  909.0 7.7 copy.67
  (132 shorter events, 65.8 us)
Async XLA Ops:
  6.5 893.3 %reduce-scatter.5.cloned.1.call-start = ((), (), s32[]{:S(2)}) async-start(), calls=%async_computation.1 | async-start | bytes 56623104 | tf_op jit(solution)/shard_map/reduce_scatter | solution.py:99
  51.2 19.0 %copy-start = (bf16[4,128,1536]{2,1,0:T(8,128)(2,1)S(1)}, bf16[4,128,1536]{2,1,0:T(8,128)(2,1)}, u32[]{:S(2)}) copy-start(bf16[4,128,1536]{2,1,0:T(8,128)(2,1)} %param.14) | copy-start | bytes 4718596
  51.2 19.0 %copy-start.1 = (s32[4,12]{1,0:T(4,128)S(1)}, s32[4,12]{1,0:T(4,128)}, u32[]{:S(2)}) copy-start(s32[4,12]{1,0:T(4,128)} %param.15) | copy-start | bytes 580
  185.3 9.1 copy-start.2
  185.3 10.3 %slice-start = ((f32[4,128,4352]{1,2,0:T(8,128)}), f32[4,128,256]{1,2,0:T(8,128)S(1)}, s32[]{:S(2)}) async-start(f32[4,128,4352]{1,2,0:T(8,128)} %copy.60), calls=%async_computation.2 | async-start | bytes 1048576 | tf_op jit(solution)/shard_map/slice | solution.py:75
Sparse Core Ops, SparseCore 0:
  614.2 285.6 reduce-scatter.4
where the time goes:
time: 926 us; the launch traced here: 924 us
  blocking collectives  304 us (33%)
  waiting for transfers between devices  286 us (31%)
  local copies, waits for them, and re-layouts  179 us (19%)
  other arithmetic  102 us (11%)
  matrix products  38 us (4%)
  between operations  14.1 us (2%)
    psum x1, blocking collectives, on_device(): occ_dens = lax.psum(partial_dens[:, :, width:], 'ao')  304 us
    reduce_scatter x1, waiting for transfers between devices, on_device(): lax.psum_scatter(panel, 'grid', scatter_dimension=0, tiled=True)  286 us
    gather x4, local copies, waits for them, and re-layouts, density(): combined[jnp.clip(local_ids, 0, nblk_local - 1)]  58.8 us
    scatter-add x4, other arithmetic, add_batch(): return (running.at[block_ids].add(contrib), None)  55.7 us
    concatenate x2, local copies, waits for them, and re-layouts, on_device(): jnp.concatenate([trial.reshape(local_rows, width), occupied.reshape(local...  44.7 us
    mul x4, other arithmetic, density(): combined[jnp.clip(local_ids, 0, nblk_local - 1)]  26.1 us
    concatenate x1, other arithmetic, on_device(): jnp.concatenate([trial.reshape(local_rows, width), occupied.reshape(local...  19 us
    dot_general x4, matrix products, project_back(): lax.dot_general(values, potential, (((0,), (0,)), ((), ())), preferred_el...  18.6 us
  transfers between devices with their start and end apart: 1, of which 1 were waited for; matrix products, arithmetic and copies ran while one was open for 0% of the time, Pallas kernels for 0%

commit v1 on v0

v1 whole, which is shorter than its diff:
```python
import functools

import jax
import jax.numpy as jnp
from jax import lax
from jax.experimental import pallas as pl
from jax.experimental.pallas import tpu as pltpu
from jax.sharding import PartitionSpec as P

F32 = jnp.float32
BF16 = jnp.bfloat16
ID_ROWS = 16
NBUF = 3
VMEM_LIMIT = 56 * 1024 * 1024


def kernel_matrix(points, quad):
    differ = points[:, :, None, :] - points[:, :, :, None]
    square = jnp.sum(differ * differ, axis=1)
    return quad[:, :, None] * quad[:, None, :] / jnp.sqrt(square + 0.25)


def spec(space):
    return pl.BlockSpec(memory_space=space)


def density_kernel(sizes, ids, meta, trial, occupied, values, keep, send, todo, rows, acc, acc_occ, sems):
    first, count, sig, blk, nvec, nv, nlocal = sizes
    npts = values.shape[1]
    nocc = rows.shape[-1]
    base = meta[0]
    parity = meta[1]
    n = jnp.int32(0)
    for b in range(count):
        for s in range(sig):
            local = ids[first + b, s] - base
            todo[0, n] = local
            todo[1, n] = b
            todo[2, n] = s
            n = n + ((local >= 0) & (local < nlocal)).astype(jnp.int32)

    def copies(j):
        slot = lax.rem(j, NBUF)
        start = todo[0, j] * blk
        out = [
            pltpu.make_async_copy(trial.at[pl.ds(start, blk), v], rows.at[slot, v], sems.at[slot, v])
            for v in range(nvec)
        ]
        out.append(pltpu.make_async_copy(occupied.at[pl.ds(start, blk)], rows.at[slot, nvec], sems.at[slot, nvec]))
        return out

    def fetch(j):
        @pl.when(j < n)
        def _():
            for c in copies(j):
                c.start()

    for j in range(NBUF - 1):
        fetch(jnp.int32(j))
    acc[...] = jnp.zeros_like(acc)
    acc_occ[...] = jnp.zeros_like(acc_occ)
    ao = lax.broadcasted_iota(jnp.int32, (blk, 2 * blk), 0)
    col = lax.broadcasted_iota(jnp.int32, (blk, 2 * blk), 1)
    spread = [(col == 2 * ao + c).astype(F32).astype(BF16) for c in range(2)]

    def step(j, carry):
        slot = lax.rem(j, NBUF)
        b = todo[1, j]
        start = pl.multiple_of(todo[2, j] * blk, blk)
        x = values[b, :, pl.ds(start, blk)]
        both = jnp.concatenate(
            [jnp.dot(x, spread[c], preferred_element_type=F32).astype(BF16) for c in range(2)], axis=0
        )
        fetch(j + NBUF - 1)
        waits = copies(j)
        for pair in range(nvec // 2):
            waits[2 * pair].wait()
            waits[2 * pair + 1].wait()
            two = jnp.concatenate([rows[slot, 2 * pair + k].reshape(2 * blk, nocc) for k in range(2)], axis=1)
            acc[b, pair] += jnp.dot(both, two, preferred_element_type=F32)
        waits[nvec].wait()
        acc_occ[b] += jnp.dot(both, rows[slot, nvec].reshape(2 * blk, nocc), preferred_element_type=F32)
        return carry

    lax.fori_loop(0, n, step, 0)
    nkeep = nvec // nv // 2
    for b in range(count):
        for q in range(nkeep):
            for half in range(nv // 2):
                for ref, bit in ((keep, parity), (send, 1 - parity)):
                    part = acc[b, (2 * q + bit) * (nv // 2) + half]
                    for k in range(2):
                        for c in range(2):
                            piece = part[c * npts : (c + 1) * npts, k * nocc : (k + 1) * nocc]
                            ref[b, q * nv + 2 * half + k, c] = piece.astype(ref.dtype)
        for ref in (keep, send):
            for c in range(2):
                ref[b, nkeep * nv, c] = acc_occ[b, c * npts : (c + 1) * npts].astype(ref.dtype)


def density(trial, occupied, colloc, blocks, meta, chunk, count, nv):
    sig = blocks.shape[1]
    npts = colloc.shape[1]
    blk = colloc.shape[2] // sig
    nvec, nocc = trial.shape[1], trial.shape[3]
    sizes = (chunk * count, count, sig, blk, nvec, nv, trial.shape[0] // blk)
    shape = (count, nvec // 2 + 1, 2, npts, nocc)
    return pl.pallas_call(
        functools.partial(density_kernel, sizes),
        grid=(1,),
        out_shape=(jax.ShapeDtypeStruct(shape, F32), jax.ShapeDtypeStruct(shape, BF16)),
        in_specs=[
            spec(pltpu.SMEM),
            spec(pltpu.SMEM),
            spec(pl.ANY),
            spec(pl.ANY),
            pl.BlockSpec((count, npts, colloc.shape[2]), lambda i: (chunk, 0, 0)),
        ],
        out_specs=(
            pl.BlockSpec(shape, lambda i: (0, 0, 0, 0, 0)),
            pl.BlockSpec(shape, lambda i: (0, 0, 0, 0, 0)),
        ),
        scratch_shapes=[
            pltpu.SMEM((3, count * sig + 1), jnp.int32),
            pltpu.VMEM((NBUF, nvec + 1, blk, 2, nocc), BF16),
            pltpu.VMEM((count, nvec // 2, 2 * npts, 2 * nocc), F32),
            pltpu.VMEM((count, 2 * npts, nocc), F32),
            pltpu.SemaphoreType.DMA((NBUF, nvec + 1)),
        ],
        compiler_params=pltpu.CompilerParams(vmem_limit_bytes=VMEM_LIMIT),
        name="density",
    )(blocks, meta, trial, occupied, colloc)


def merge_kernel(nv, bit, held, received, keep, send):
    nkeep = (keep.shape[1] - 1) // nv
    mine = bit[0]
    for b in range(keep.shape[0]):
        for q in range(nkeep):
            for v in range(nv):
                for ref, which in ((keep, mine), (send, 1 - mine)):
                    at = (2 * q + which) * nv + v
                    ref[b, q * nv + v] = (held[b, at] + received[b, at].astype(F32)).astype(ref.dtype)
        total = held[b, 2 * nkeep * nv] + received[b, 2 * nkeep * nv].astype(F32)
        keep[b, nkeep * nv] = total
        send[b, nkeep * nv] = total.astype(BF16)


def merge(held, received, bit, nv):
    shape = (held.shape[0], (held.shape[1] - 1) // 2 + 1) + held.shape[2:]
    return pl.pallas_call(
        functools.partial(merge_kernel, nv),
        out_shape=(jax.ShapeDtypeStruct(shape, F32), jax.ShapeDtypeStruct(shape, BF16)),
        in_specs=[spec(pltpu.SMEM), spec(pltpu.VMEM), spec(pltpu.VMEM)],
        out_specs=(spec(pltpu.VMEM), spec(pltpu.VMEM)),
        compiler_params=pltpu.CompilerParams(vmem_limit_bytes=VMEM_LIMIT),
        name="merge",
    )(bit, held, received)


def exchange_kernel(first, held, received, kern, *refs):
    outs, (left, stack) = refs[:-2], refs[-2:]
    nv = held.shape[1] - 1
    npts, nocc = held.shape[3], held.shape[4]
    per_out = outs[0].shape[0]
    dims = (((1,), (1,)), ((), ()))
    for b in range(held.shape[0]):
        total = lambda u, c: (held[b, u, c] + received[b, u, c].astype(F32)).astype(BF16)
        oreal, oimag = total(nv, 0), total(nv, 1)
        turn = jnp.concatenate(
            [
                jnp.concatenate([oreal, oimag], axis=1),
                jnp.concatenate([-oimag, oreal], axis=1),
            ],
            axis=0,
        )
        for v in range(nv):
            for c in range(2):
                left[v * npts : (v + 1) * npts, c * nocc : (c + 1) * nocc] = total(v, c)
        rho = lax.dot_general(left[...], turn, dims, preferred_element_type=F32)
        weight = kern[first + b]
        weight = jnp.concatenate([weight, weight], axis=1)
        for v in range(nv):
            stack[v * npts : (v + 1) * npts] = (rho[v * npts : (v + 1) * npts] * weight).astype(BF16)
        result = jnp.dot(stack[...], turn, preferred_element_type=F32).astype(BF16)
        for v in range(nv):
            outs[b // per_out][b % per_out, :, v * 2 * nocc : (v + 1) * 2 * nocc] = result[v * npts : (v + 1) * npts]


def exchange(held, received, kern, chunk):
    count, nv, npts, nocc = held.shape[0], held.shape[1] - 1, held.shape[3], held.shape[4]
    out = jax.ShapeDtypeStruct((count // 2, npts, nv * 2 * nocc), BF16)
    return pl.pallas_call(
        functools.partial(exchange_kernel, chunk * count),
        out_shape=(out, out),
        in_specs=[spec(pltpu.VMEM)] * 3,
        out_specs=(spec(pltpu.VMEM),) * 2,
        scratch_shapes=[pltpu.VMEM((nv * npts, 2 * nocc), BF16), pltpu.VMEM((nv * npts, 2 * npts), BF16)],
        compiler_params=pltpu.CompilerParams(vmem_limit_bytes=VMEM_LIMIT),
        name="exchange",
    )(held, received, kern)


def project_kernel(sizes, ids, meta, *refs):
    npieces, nown, sig, blk, npts, has_acc, last = sizes
    at = 2 * npieces
    values, potentials = refs[:npieces], refs[npieces:at]
    before = refs[at] if has_acc else None
    out = refs[at + has_acc]
    x, e, acc, sems = refs[at + has_acc + 1 :]
    base = meta[2]
    copies = []
    place = 0
    for i in range(npieces):
        size = values[i].shape[0]
        copies.append(
            pltpu.make_async_copy(values[i].at[:, pl.ds(0, npts)], x.at[pl.ds(place, size)], sems.at[2 * i])
        )
        copies.append(pltpu.make_async_copy(potentials[i], e.at[pl.ds(place, size)], sems.at[2 * i + 1]))
        place += size
    if has_acc:
        copies.append(pltpu.make_async_copy(before, acc, sems.at[2 * npieces]))
    for c in copies:
        c.start()
    if not has_acc:
        acc[...] = jnp.zeros_like(acc)
    for c in copies:
        c.wait()

    def one(i, carry):
        for s in range(sig):
            own = ids[i, s] - base

            @pl.when((own >= 0) & (own < nown))
            def _():
                acc[own] += lax.dot_general(
                    x[i, :, s * blk : (s + 1) * blk], e[i], (((0,), (0,)), ((), ())), preferred_element_type=F32
                )

        return carry

    lax.fori_loop(0, place, one, 0)
    if last:
        nocc = out.shape[2]
        for o in range(nown):
            for v in range(out.shape[0]):
                for c in range(2):
                    col = (2 * v + c) * nocc
                    out[v, pl.ds(o * 2 * blk + c, blk, stride=2), :] = acc[o, :, col : col + nocc]
    else:
        out[...] = acc[...]


def project(values, potentials, ids, meta, before, last, nown, nv, blk, npts, nocc):
    width = nv * 2 * nocc
    total = ids.shape[0]
    sig = ids.shape[1]
    n = len(values)
    has_acc = before is not None
    sizes = (n, nown, sig, blk, npts, int(has_acc), last)
    shape = (nv, nown * blk * 2, nocc) if last else (nown, blk, width)
    args = [ids, meta, *values, *potentials] + ([before] if has_acc else [])
    return pl.pallas_call(
        functools.partial(project_kernel, sizes),
        out_shape=jax.ShapeDtypeStruct(shape, F32),
        in_specs=[spec(pltpu.SMEM)] * 2 + [spec(pl.ANY)] * (2 * n + int(has_acc)),
        out_specs=spec(pltpu.VMEM),
        scratch_shapes=[
            pltpu.VMEM((total, npts, sig * blk), BF16),
            pltpu.VMEM((total, npts, width), BF16),
            pltpu.VMEM((nown, blk, width), F32),
            pltpu.SemaphoreType.DMA((2 * n + 1,)),
        ],
        compiler_params=pltpu.CompilerParams(vmem_limit_bytes=VMEM_LIMIT),
        name="project",
    )(*args)


def swap(array, axis, bit):
    size = lax.axis_size(axis)
    return lax.ppermute(array, axis, [(i, i ^ bit) for i in range(size)])


def gather_all(part, reverse):
    bits = [1 << b for b in range(1, lax.axis_size("grid").bit_length() - 1)]
    if reverse:
        bits = bits[::-1]
    held = part
    for i, bit in enumerate(bits):
        got = swap(held, "grid", bit)
        if i + 1 < len(bits):
            held = jnp.concatenate([held, got], axis=0)
    pieces = [held, got]
    return pieces + [swap(p, "grid", 1) for p in pieces]


def on_device(trial, occupied, colloc, blocks, coords, weights):
    n_ao, n_grid = lax.axis_size("ao"), lax.axis_size("grid")
    batches, npts, _ = colloc.shape
    sig = blocks.shape[1]
    blk = colloc.shape[2] // sig
    nvec, nocc = trial.shape[1], trial.shape[3]
    nv = nvec // n_ao
    nlocal = trial.shape[0] // blk
    nown = nlocal * n_ao // n_grid
    count = batches // 2
    ao, grid = lax.axis_index("ao"), lax.axis_index("grid")
    meta = jnp.stack([ao * nlocal, ao & 1, grid * nown]).astype(jnp.int32)
    steps = n_ao.bit_length() - 1

    numbers = jnp.stack([blocks % 128, blocks // 128], axis=1).astype(BF16)
    numbers = jnp.pad(numbers, ((0, 0), (0, ID_ROWS - 2), (0, colloc.shape[2] - sig)))
    payload = jnp.concatenate([colloc, numbers], axis=1)
    half = count // 2
    values = []
    for chunk in range(2):
        pieces = []
        for h in range(2):
            at = chunk * count + h * half
            pieces += gather_all(payload[at : at + half], h == 1)
        values.append(pieces)
    kern = kernel_matrix(coords, weights)

    total = None
    for chunk in range(2):
        keep, send = density(trial, occupied, colloc, blocks, meta, chunk, count, nv)
        for s in range(steps):
            got = swap(send, "ao", 1 << s)
            if s + 1 < steps:
                bit = ((ao >> (s + 1)) & 1).astype(jnp.int32).reshape(1)
                keep, send = merge(keep, got, bit, nv)
        parts = exchange(keep, got, kern, chunk)
        potentials = []
        for h in range(2):
            potentials += gather_all(parts[h], h == 1)
        numbers = jnp.concatenate([p[:, npts : npts + 2, :sig] for p in values[chunk]], axis=0).astype(jnp.int32)
        ids = numbers[:, 0] + 128 * numbers[:, 1]
        total = project(
            values[chunk], potentials, ids, meta, total, chunk == 1, nown, nv, blk, npts, nocc
        )
    return total.reshape(nv, nown * blk, 2, nocc)


def solution(mesh):
    in_specs = (
        P("ao", None, None, None),
        P("ao", None, None),
        P("grid", None, None),
        P("grid", None),
        P("grid", None, None),
        P("grid", None),
    )
    out_specs = P("ao", "grid", None, None)
    return jax.shard_map(on_device, mesh=mesh, in_specs=in_specs, out_specs=out_specs, check_vma=False)
```

time: 926 us -> 269 us (0.29)
  blocking collectives: 304 us -> 0 us
  waiting for transfers between devices: 286 us -> 91.4 us
  local copies, waits for them, and re-layouts: 179 us -> 9.85 us
  Pallas kernels: 0 us -> 151 us
  other arithmetic: 102 us -> 5.6 us
  matrix products: 38 us -> 0 us
  between operations: 14.1 us -> 0.8 us
  starting transfers between devices: 0.01 us -> 9.66 us
    psum x1 -> x0, blocking collectives: 304 us -> none  [on_device(): occ_dens = lax.psum(partial_dens[:, :, width:], 'ao')]
    reduce_scatter x1 -> x0, waiting for transfers between devices: 286 us -> none  [on_device(): lax.psum_scatter(panel, 'grid', scatter_dimension=0, tiled=True)]
    pallas_call x0 -> x8, Pallas kernels: none -> 151 us  [the longest x2 99.8 us: density(): pl.pallas_call(functools.partial(density_kernel, sizes), grid=(1,), out_s...]
    ppermute x0 -> x36, waiting for transfers between devices: none -> 91.4 us  [swap(): return lax.ppermute(array, axis, [(i, i ^ bit) for i in range(size)])]
    gather x4 -> x0, local copies, waits for them, and re-layouts: 58.8 us -> none  [density(): combined[jnp.clip(local_ids, 0, nblk_local - 1)]]
    scatter-add x4 -> x0, other arithmetic: 55.7 us -> none  [add_batch(): return (running.at[block_ids].add(contrib), None)]
    concatenate x2 -> x6, local copies, waits for them, and re-layouts: 44.7 us -> 0.1 us  [the longest x4 0.08 us: gather_all(): held = jnp.concatenate([held, got], axis=0)]
    dot_general x40 -> x0, matrix products: 38 us -> none  [the longest x4 18.6 us: project_back(): lax.dot_general(values, potential, (((0,), (0,)), ((), ())), preferred_el...]
  transfers between devices with their start and end apart: 1 -> 36, of which waited for: 1 -> 13; matrix products, arithmetic and copies ran while one was open for 0% -> 4% of each run, Pallas kernels for 0% -> 48%
where the time goes in v1:
time: 269 us
  Pallas kernels  151 us (56%)
  waiting for transfers between devices  91.4 us (34%)
  local copies, waits for them, and re-layouts  9.85 us (4%)
  starting transfers between devices  9.66 us (4%)
  other arithmetic  5.6 us (2%)
    pallas_call x2, Pallas kernels, density(): pl.pallas_call(functools.partial(density_kernel, sizes), grid=(1,), out_s...  99.8 us
    ppermute x36, waiting for transfers between devices, swap(): return lax.ppermute(array, axis, [(i, i ^ bit) for i in range(size)])  91.4 us
    pallas_call x2, Pallas kernels, project(): pl.pallas_call(functools.partial(project_kernel, sizes), out_shape=jax.Sh...  37.9 us
    unnamed x75, local copies, waits for them, and re-layouts  9.75 us
    ppermute x36, starting transfers between devices, swap(): return lax.ppermute(array, axis, [(i, i ^ bit) for i in range(size)])  9.66 us
    pallas_call x2, Pallas kernels, merge(): pl.pallas_call(functools.partial(merge_kernel, nv), out_shape=(jax.ShapeD...  7.56 us
    pallas_call x2, Pallas kernels, exchange(): pl.pallas_call(functools.partial(exchange_kernel, chunk * count), out_sha...  5.97 us
  transfers between devices with their start and end apart: 36, of which 13 were waited for; matrix products, arithmetic and copies ran while one was open for 4% of the time, Pallas kernels for 48%

profile of v1, /device:TPU:0, one launch (start us, length us, event | category | flops | bytes accessed | tf_op | source)
XLA Modules:
  0.0 268.5 jit_solution(12539400680425238671)
XLA Ops:
  0.7 1.5 pad_maximum_fusion.4
  2.2 3.0 %collective-permute-start.18 = (bf16[1,144,1536]{2,1,0:T(8,128)(2,1)S(1)}, bf16[1,144,1536]{2,1,0:T(8,128)(2,1)S(1)}, u32[]{:S(2)}, u32[]{:S(2)}) collective-permute-start(bf16[1,144,1536]{2,1,0:T(8,128)(2,1)S(1)} %get-tuple-element.32), channel_id=1, source_target_pairs={{0,8},{4,12},{8,0},{12,4},{16,24},{20,28},{24,16},{28,20},{1,9},{5... | collective-permute-start | bytes 1327112 | tf_op jit(solution)/shard_map/ppermute | solution.py:281
  5.9 50.9 %density.3 = (f32[2,9,2,128,128]{4,3,2,1,0:T(8,128)}, bf16[2,9,2,128,128]{4,3,2,1,0:T(8,128)(2,1)}) custom-call(s32[4,12]{1,0:T(4,128)} %ids.3, s32[3]{0:T(128)} %pad_add_fusion.meta, bf16[3072,16,2,128]{3,2,1,0:T(2,128)(2,1)} %trial.3, bf16[3072,2,128]{2,1,0:T(2,128)(2,1)} %occupied.3, bf16[4,128,1536]{2,1,0:T(8,128)(2,1)} %values.3), custom_call_target="tpu_custom_call" | custom-call | tf_op jit(solution)/shard_map/density/pallas_call | solution.py:108
  57.2 48.9 %density.2 = (f32[2,9,2,128,128]{4,3,2,1,0:T(8,128)}, bf16[2,9,2,128,128]{4,3,2,1,0:T(8,128)(2,1)}) custom-call(s32[4,12]{1,0:T(4,128)} %ids.3, s32[3]{0:T(128)} %pad_add_fusion.meta, bf16[3072,16,2,128]{3,2,1,0:T(2,128)(2,1)} %trial.3, bf16[3072,2,128]{2,1,0:T(2,128)(2,1)} %occupied.3, bf16[4,128,1536]{2,1,0:T(8,128)(2,1)} %values.3), custom_call_target="tpu_custom_call" | custom-call | tf_op jit(solution)/shard_map/density/pallas_call | solution.py:108
  107.4 2.1 collective-permute-start.19
  109.9 3.8 %merge.3 = (f32[2,5,2,128,128]{4,3,2,1,0:T(8,128)}, bf16[2,5,2,128,128]{4,3,2,1,0:T(8,128)(2,1)}) custom-call(s32[1]{0:T(128)} %bitcast.6.bit, f32[2,9,2,128,128]{4,3,2,1,0:T(8,128)} %get-tuple-element.23.held, bf16[2,9,2,128,128]{4,3,2,1,0:T(8,128)(2,1)} %collective-permute-done.26.received), custom_call_target="tpu_custom_call" | custom-call | tf_op jit(solution)/shard_map/merge/pallas_call | solution.py:151
  113.6 4.6 %collective-permute-done.4 = bf16[1,144,1536]{2,1,0:T(8,128)(2,1)S(1)} collective-permute-done((bf16[1,144,1536]{2,1,0:T(8,128)(2,1)S(1)}, bf16[1,144,1536]{2,1,0:T(8,128)(2,1)S(1)}, u32[]{:S(2)}, u32[]{:S(2)}) %collective-permute-start.4) | collective-permute-done | bytes 442400 | tf_op jit(solution)/shard_map/ppermute | solution.py:281
  118.2 4.4 %collective-permute-done.8.received = bf16[2,9,2,128,128]{4,3,2,1,0:T(8,128)(2,1)} collective-permute-done((bf16[2,9,2,128,128]{4,3,2,1,0:T(8,128)(2,1)}, bf16[2,9,2,128,128]{4,3,2,1,0:T(8,128)(2,1)}, u32[]{:S(2)}, u32[]{:S(2)}) %collective-permute-start.8) | collective-permute-done | bytes 1179680 | tf_op jit(solution)/shard_map/ppermute | solution.py:281
  122.7 3.8 %merge.2 = (f32[2,5,2,128,128]{4,3,2,1,0:T(8,128)}, bf16[2,5,2,128,128]{4,3,2,1,0:T(8,128)(2,1)}) custom-call(s32[1]{0:T(128)} %bitcast.6.bit, f32[2,9,2,128,128]{4,3,2,1,0:T(8,128)} %get-tuple-element.17.held, bf16[2,9,2,128,128]{4,3,2,1,0:T(8,128)(2,1)} %collective-permute-done.8.received), custom_call_target="tpu_custom_call" | custom-call | tf_op jit(solution)/shard_map/merge/pallas_call | solution.py:151
  126.5 8.1 %collective-permute-done.19.refs_1_ = bf16[2,144,1536]{2,1,0:T(8,128)(2,1)} collective-permute-done((bf16[2,144,1536]{2,1,0:T(8,128)(2,1)S(1)}, bf16[2,144,1536]{2,1,0:T(8,128)(2,1)}, u32[]{:S(2)}, u32[]{:S(2)}) %collective-permute-start.19) | collective-permute-done | bytes 884768 | tf_op jit(solution)/shard_map/ppermute | solution.py:281
  136.0 30.1 %collective-permute-done.27.received = bf16[2,5,2,128,128]{4,3,2,1,0:T(8,128)(2,1)S(1)} collective-permute-done((bf16[2,5,2,128,128]{4,3,2,1,0:T(8,128)(2,1)}, bf16[2,5,2,128,128]{4,3,2,1,0:T(8,128)(2,1)S(1)}, u32[]{:S(2)}, u32[]{:S(2)}) %collective-permute-start.27) | collective-permute-done | bytes 655392 | tf_op jit(solution)/shard_map/ppermute | solution.py:281
  166.9 3.0 %exchange.3 = (bf16[1,128,1024]{2,1,0:T(8,128)(2,1)}, bf16[1,128,1024]{2,1,0:T(8,128)(2,1)}) custom-call(f32[2,5,2,128,128]{4,3,2,1,0:T(8,128)} %get-tuple-element.25.held, bf16[2,5,2,128,128]{4,3,2,1,0:T(8,128)(2,1)} %copy-done.15, f32[4,128,128]{2,1,0:T(8,128)} %rsqrt_multiply_fusion.kern), custom_call_target="tpu_custom_call" | custom-call | tf_op jit(solution)/shard_map/exchange/pallas_call | solution.py:193
  170.7 1.2 collective-permute-start.28
  172.0 6.6 %collective-permute-done.9.received = bf16[2,5,2,128,128]{4,3,2,1,0:T(8,128)(2,1)S(1)} collective-permute-done((bf16[2,5,2,128,128]{4,3,2,1,0:T(8,128)(2,1)}, bf16[2,5,2,128,128]{4,3,2,1,0:T(8,128)(2,1)S(1)}, u32[]{:S(2)}, u32[]{:S(2)}) %collective-permute-start.9) | collective-permute-done | bytes 655392 | tf_op jit(solution)/shard_map/ppermute | solution.py:281
  179.5 3.0 %exchange.2 = (bf16[1,128,1024]{2,1,0:T(8,128)(2,1)}, bf16[1,128,1024]{2,1,0:T(8,128)(2,1)}) custom-call(f32[2,5,2,128,128]{4,3,2,1,0:T(8,128)} %get-tuple-element.19.held, bf16[2,5,2,128,128]{4,3,2,1,0:T(8,128)(2,1)} %copy-done.14, f32[4,128,128]{2,1,0:T(8,128)} %rsqrt_multiply_fusion.kern), custom_call_target="tpu_custom_call" | custom-call | tf_op jit(solution)/shard_map/exchange/pallas_call | solution.py:193
  182.5 8.7 %collective-permute-done.28 = bf16[1,128,1024]{2,1,0:T(8,128)(2,1)S(1)} collective-permute-done((bf16[1,128,1024]{2,1,0:T(8,128)(2,1)}, bf16[1,128,1024]{2,1,0:T(8,128)(2,1)S(1)}, u32[]{:S(2)}, u32[]{:S(2)}) %collective-permute-start.28) | collective-permute-done | bytes 262176 | tf_op jit(solution)/shard_map/ppermute | solution.py:281
  192.3 1.0 constant_dynamic-update-slice_fusion.9
  193.3 4.5 %collective-permute-done.10 = bf16[1,128,1024]{2,1,0:T(8,128)(2,1)S(1)} collective-permute-done((bf16[1,128,1024]{2,1,0:T(8,128)(2,1)}, bf16[1,128,1024]{2,1,0:T(8,128)(2,1)S(1)}, u32[]{:S(2)}, u32[]{:S(2)}) %collective-permute-start.10) | collective-permute-done | bytes 262176 | tf_op jit(solution)/shard_map/ppermute | solution.py:281
  202.9 1.1 collective-permute-done.7.refs_7_
  204.0 10.6 %collective-permute-done.33.refs_13_ = bf16[2,128,1024]{2,1,0:T(8,128)(2,1)S(1)} collective-permute-done((bf16[2,128,1024]{2,1,0:T(8,128)(2,1)S(1)}, bf16[2,128,1024]{2,1,0:T(8,128)(2,1)S(1)}, u32[]{:S(2)}, u32[]{:S(2)}) %collective-permute-start.33) | collective-permute-done | bytes 524320 | tf_op jit(solution)/shard_map/ppermute | solution.py:281
  215.4 9.5 %collective-permute-done.15.refs_13_ = bf16[2,128,1024]{2,1,0:T(8,128)(2,1)S(1)} collective-permute-done((bf16[2,128,1024]{2,1,0:T(8,128)(2,1)S(1)}, bf16[2,128,1024]{2,1,0:T(8,128)(2,1)S(1)}, u32[]{:S(2)}, u32[]{:S(2)}) %collective-permute-start.15) | collective-permute-done | bytes 524320 | tf_op jit(solution)/shard_map/ppermute | solution.py:281
  225.0 1.8 collective-permute-done.11.refs_9_
  229.4 15.8 %project.2.refs_16_ = f32[12,128,1024]{2,1,0:T(8,128)} custom-call(s32[16,12]{1,0:T(8,128)} %bitcast.12, s32[3]{0:T(128)} %pad_add_fusion.meta, bf16[2,144,1536]{2,1,0:T(8,128)(2,1)} %copy-done.1, bf16[2,144,1536]{2,1,0:T(8,128)(2,1)} %collective-permute-done.19.refs_1_, bf16[2,144,1536]{2,1,0:T(8,128)(2,1)} %collective-permute-done.20.refs_2_, ...), custom_call_target="tpu_custom_call" | custom-call | tf_op jit(solution)/shard_map/project/pallas_call | solution.py:263
  246.3 22.1 %project.3 = f32[4,3072,128]{2,1,0:T(8,128)} custom-call(s32[16,12]{1,0:T(8,128)} %bitcast.11, s32[3]{0:T(128)} %pad_add_fusion.meta, bf16[2,144,1536]{2,1,0:T(8,128)(2,1)} %copy-done, bf16[2,144,1536]{2,1,0:T(8,128)(2,1)} %collective-permute-done.1.refs_1_, bf16[2,144,1536]{2,1,0:T(8,128)(2,1)} %copy-done.8, bf16[2,144,1536]{2,1,0:T(8,128)(2,1)} %copy-done.9, ...), custom_call_target="tpu_custom_call" | custom-call | tf_op jit(solution)/shard_map/project/pallas_call | solution.py:263
  (157 shorter events, 17.7 us)
Async XLA Ops:
  2.2 105.0 %collective-permute-start.18 = (bf16[1,144,1536]{2,1,0:T(8,128)(2,1)S(1)}, bf16[1,144,1536]{2,1,0:T(8,128)(2,1)S(1)}, u32[]{:S(2)}, u32[]{:S(2)}) collective-permute-start(bf16[1,144,1536]{2,1,0:T(8,128)(2,1)S(1)} %get-tuple-element.32), channel_id=1, source_target_pairs={{0,8},{4,12},{8,0},{12,4},{16,24},{20,28},{24,16},{28,20},{1,9},{5... | collective-permute-start | bytes 1327112 | tf_op jit(solution)/shard_map/ppermute | solution.py:281
  56.9 52.9 %collective-permute-start.26 = (bf16[2,9,2,128,128]{4,3,2,1,0:T(8,128)(2,1)}, bf16[2,9,2,128,128]{4,3,2,1,0:T(8,128)(2,1)}, u32[]{:S(2)}, u32[]{:S(2)}) collective-permute-start(bf16[2,9,2,128,128]{4,3,2,1,0:T(8,128)(2,1)} %get-tuple-element.24), channel_id=1, source_target_pairs={{0,1},{1,0},{2,3},{3,2},{4,5},{5,4},{6,7},{7,6},{8,9},{9,8},{10,11... | collective-permute-start | bytes 3538952 | tf_op jit(solution)/shard_map/ppermute | solution.py:281
  57.0 50.4 %collective-permute-start.22 = (bf16[1,144,1536]{2,1,0:T(8,128)(2,1)S(1)}, bf16[1,144,1536]{2,1,0:T(8,128)(2,1)S(1)}, u32[]{:S(2)}, u32[]{:S(2)}) collective-permute-start(bf16[1,144,1536]{2,1,0:T(8,128)(2,1)S(1)} %get-tuple-element.29), channel_id=1, source_target_pairs={{0,16},{4,20},{8,24},{12,28},{16,0},{20,4},{24,8},{28,12},{1,17},{... | collective-permute-start | bytes 1327112 | tf_op jit(solution)/shard_map/ppermute | solution.py:281
  57.1 52.5 %collective-permute-start = (bf16[1,144,1536]{2,1,0:T(8,128)(2,1)S(1)}, bf16[1,144,1536]{2,1,0:T(8,128)(2,1)S(1)}, u32[]{:S(2)}, u32[]{:S(2)}) collective-permute-start(bf16[1,144,1536]{2,1,0:T(8,128)(2,1)S(1)} %get-tuple-element.30), channel_id=1, source_target_pairs={{0,8},{4,12},{8,0},{12,4},{16,24},{20,28},{24,16},{28,20},{1,9},{5... | collective-permute-start | bytes 1327112 | tf_op jit(solution)/shard_map/ppermute | solution.py:281
  106.0 16.6 %collective-permute-start.8 = (bf16[2,9,2,128,128]{4,3,2,1,0:T(8,128)(2,1)}, bf16[2,9,2,128,128]{4,3,2,1,0:T(8,128)(2,1)}, u32[]{:S(2)}, u32[]{:S(2)}) collective-permute-start(bf16[2,9,2,128,128]{4,3,2,1,0:T(8,128)(2,1)} %get-tuple-element.18), channel_id=1, source_target_pairs={{0,1},{1,0},{2,3},{3,2},{4,5},{5,4},{6,7},{7,6},{8,9},{9,8},{10,11... | collective-permute-start | bytes 3538952 | tf_op jit(solution)/shard_map/ppermute | solution.py:281
  107.4 27.3 %collective-permute-start.19 = (bf16[2,144,1536]{2,1,0:T(8,128)(2,1)S(1)}, bf16[2,144,1536]{2,1,0:T(8,128)(2,1)}, u32[]{:S(2)}, u32[]{:S(2)}) collective-permute-start(bf16[2,144,1536]{2,1,0:T(8,128)(2,1)S(1)} %pad_maximum_fusion.2.refs_0_), channel_id=1, source_target_pairs={{0,16},{4,20},{8,24},{12,28},{16,0},{20,4},{24,8},{28,12},{1,17},{... | collective-permute-start | bytes 2654216 | tf_op jit(solution)/shard_map/ppermute | solution.py:281
  109.6 25.8 %collective-permute-start.20 = (bf16[2,144,1536]{2,1,0:T(8,128)(2,1)S(1)}, bf16[2,144,1536]{2,1,0:T(8,128)(2,1)}, u32[]{:S(2)}, u32[]{:S(2)}) collective-permute-start(bf16[2,144,1536]{2,1,0:T(8,128)(2,1)S(1)} %pad_maximum_fusion.2.refs_0_), channel_id=1, source_target_pairs={{0,4},{4,0},{8,12},{12,8},{16,20},{20,16},{24,28},{28,24},{1,5},{5... | collective-permute-start | bytes 2654216 | tf_op jit(solution)/shard_map/ppermute | solution.py:281
  109.8 60.2 %collective-permute-start.1 = (bf16[2,144,1536]{2,1,0:T(8,128)(2,1)S(1)}, bf16[2,144,1536]{2,1,0:T(8,128)(2,1)}, u32[]{:S(2)}, u32[]{:S(2)}) collective-permute-start(bf16[2,144,1536]{2,1,0:T(8,128)(2,1)S(1)} %pad_maximum_fusion.refs_0_), channel_id=1, source_target_pairs={{0,16},{4,20},{8,24},{12,28},{16,0},{20,4},{24,8},{28,12},{1,17},{... | collective-permute-start | bytes 2654216 | tf_op jit(solution)/shard_map/ppermute | solution.py:281
  118.2 52.5 %collective-permute-start.2 = (bf16[2,144,1536]{2,1,0:T(8,128)(2,1)S(1)}, bf16[2,144,1536]{2,1,0:T(8,128)(2,1)S(1)}, u32[]{:S(2)}, u32[]{:S(2)}) collective-permute-start(bf16[2,144,1536]{2,1,0:T(8,128)(2,1)S(1)} %pad_maximum_fusion.refs_0_), channel_id=1, source_target_pairs={{0,4},{4,0},{8,12},{12,8},{16,20},{20,16},{24,28},{28,24},{1,5},{5... | collective-permute-start | bytes 2654216 | tf_op jit(solution)/shard_map/ppermute | solution.py:281
  122.6 43.5 %collective-permute-start.27 = (bf16[2,5,2,128,128]{4,3,2,1,0:T(8,128)(2,1)}, bf16[2,5,2,128,128]{4,3,2,1,0:T(8,128)(2,1)S(1)}, u32[]{:S(2)}, u32[]{:S(2)}) collective-permute-start(bf16[2,5,2,128,128]{4,3,2,1,0:T(8,128)(2,1)} %get-tuple-element.26), channel_id=1, source_target_pairs={{0,2},{1,3},{2,0},{3,1},{4,6},{5,7},{6,4},{7,5},{8,10},{9,11},{10,... | collective-permute-start | bytes 1966088 | tf_op jit(solution)/shard_map/ppermute | solution.py:281
  134.6 63.3 %collective-permute-start.23 = (bf16[2,144,1536]{2,1,0:T(8,128)(2,1)S(1)}, bf16[2,144,1536]{2,1,0:T(8,128)(2,1)}, u32[]{:S(2)}, u32[]{:S(2)}) collective-permute-start(bf16[2,144,1536]{2,1,0:T(8,128)(2,1)S(1)} %pad_maximum_fusion.3.refs_4_), channel_id=1, source_target_pairs={{0,8},{4,12},{8,0},{12,4},{16,24},{20,28},{24,16},{28,20},{1,9},{5... | collective-permute-start | bytes 2654216 | tf_op jit(solution)/shard_map/ppermute | solution.py:281
  135.3 43.3 %collective-permute-start.9 = (bf16[2,5,2,128,128]{4,3,2,1,0:T(8,128)(2,1)}, bf16[2,5,2,128,128]{4,3,2,1,0:T(8,128)(2,1)S(1)}, u32[]{:S(2)}, u32[]{:S(2)}) collective-permute-start(bf16[2,5,2,128,128]{4,3,2,1,0:T(8,128)(2,1)} %get-tuple-element.20), channel_id=1, source_target_pairs={{0,2},{1,3},{2,0},{3,1},{4,6},{5,7},{6,4},{7,5},{8,10},{9,11},{10,... | collective-permute-start | bytes 1966088 | tf_op jit(solution)/shard_map/ppermute | solution.py:281
  166.1 32.4 %collective-permute-start.5 = (bf16[2,144,1536]{2,1,0:T(8,128)(2,1)S(1)}, bf16[2,144,1536]{2,1,0:T(8,128)(2,1)}, u32[]{:S(2)}, u32[]{:S(2)}) collective-permute-start(bf16[2,144,1536]{2,1,0:T(8,128)(2,1)S(1)} %pad_maximum_fusion.1.refs_4_), channel_id=1, source_target_pairs={{0,8},{4,12},{8,0},{12,4},{16,24},{20,28},{24,16},{28,20},{1,9},{5... | collective-permute-start | bytes 2654216 | tf_op jit(solution)/shard_map/ppermute | solution.py:281
  170.7 20.5 %collective-permute-start.28 = (bf16[1,128,1024]{2,1,0:T(8,128)(2,1)}, bf16[1,128,1024]{2,1,0:T(8,128)(2,1)S(1)}, u32[]{:S(2)}, u32[]{:S(2)}) collective-permute-start(bf16[1,128,1024]{2,1,0:T(8,128)(2,1)} %get-tuple-element.27), channel_id=1, source_target_pairs={{0,8},{4,12},{8,0},{12,4},{16,24},{20,28},{24,16},{28,20},{1,9},{5... | collective-permute-start | bytes 786440 | tf_op jit(solution)/shard_map/ppermute | solution.py:281
  178.6 20.0 %collective-permute-start.21 = (bf16[2,144,1536]{2,1,0:T(8,128)(2,1)}, bf16[2,144,1536]{2,1,0:T(8,128)(2,1)}, u32[]{:S(2)}, u32[]{:S(2)}) collective-permute-start(bf16[2,144,1536]{2,1,0:T(8,128)(2,1)} %collective-permute-done.19.refs_1_), channel_id=1, source_target_pairs={{0,4},{4,0},{8,12},{12,8},{16,20},{20,16},{24,28},{28,24},{1,5},{5... | collective-permute-start | bytes 2654216 | tf_op jit(solution)/shard_map/ppermute | solution.py:281
  199.7 14.9 %collective-permute-start.33 = (bf16[2,128,1024]{2,1,0:T(8,128)(2,1)S(1)}, bf16[2,128,1024]{2,1,0:T(8,128)(2,1)S(1)}, u32[]{:S(2)}, u32[]{:S(2)}) collective-permute-start(bf16[2,128,1024]{2,1,0:T(8,128)(2,1)S(1)} %constant_dynamic-update-slice_fusion.22.refs_12_), channel_id=1, source_target_pairs={{0,8},{4,12},{8,0},{12,4},{16,24},{20,28},{24,16},{28,20},{1,9},{5... | collective-permute-start | bytes 1572872 | tf_op jit(solution)/shard_map/ppermute | solution.py:281
  200.2 14.4 %collective-permute-start.29 = (bf16[2,128,1024]{2,1,0:T(8,128)(2,1)S(1)}, bf16[2,128,1024]{2,1,0:T(8,128)(2,1)S(1)}, u32[]{:S(2)}, u32[]{:S(2)}) collective-permute-start(bf16[2,128,1024]{2,1,0:T(8,128)(2,1)S(1)} %constant_dynamic-update-slice_fusion.20.refs_8_), channel_id=1, source_target_pairs={{0,16},{4,20},{8,24},{12,28},{16,0},{20,4},{24,8},{28,12},{1,17},{... | collective-permute-start | bytes 1572872 | tf_op jit(solution)/shard_map/ppermute | solution.py:281
  201.7 13.0 %collective-permute-start.34 = (bf16[2,128,1024]{2,1,0:T(8,128)(2,1)S(1)}, bf16[2,128,1024]{2,1,0:T(8,128)(2,1)S(1)}, u32[]{:S(2)}, u32[]{:S(2)}) collective-permute-start(bf16[2,128,1024]{2,1,0:T(8,128)(2,1)S(1)} %constant_dynamic-update-slice_fusion.22.refs_12_), channel_id=1, source_target_pairs={{0,4},{4,0},{8,12},{12,8},{16,20},{20,16},{24,28},{28,24},{1,5},{5... | collective-permute-start | bytes 1572872 | tf_op jit(solution)/shard_map/ppermute | solution.py:281
  202.8 12.6 %collective-permute-start.30 = (bf16[2,128,1024]{2,1,0:T(8,128)(2,1)S(1)}, bf16[2,128,1024]{2,1,0:T(8,128)(2,1)S(1)}, u32[]{:S(2)}, u32[]{:S(2)}) collective-permute-start(bf16[2,128,1024]{2,1,0:T(8,128)(2,1)S(1)} %constant_dynamic-update-slice_fusion.20.refs_8_), channel_id=1, source_target_pairs={{0,4},{4,0},{8,12},{12,8},{16,20},{20,16},{24,28},{28,24},{1,5},{5... | collective-permute-start | bytes 1572872 | tf_op jit(solution)/shard_map/ppermute | solution.py:281
  204.0 20.9 %collective-permute-start.15 = (bf16[2,128,1024]{2,1,0:T(8,128)(2,1)S(1)}, bf16[2,128,1024]{2,1,0:T(8,128)(2,1)S(1)}, u32[]{:S(2)}, u32[]{:S(2)}) collective-permute-start(bf16[2,128,1024]{2,1,0:T(8,128)(2,1)S(1)} %constant_dynamic-update-slice_fusion.10.refs_12_), channel_id=1, source_target_pairs={{0,8},{4,12},{8,0},{12,4},{16,24},{20,28},{24,16},{28,20},{1,9},{5... | collective-permute-start | bytes 1572872 | tf_op jit(solution)/shard_map/ppermute | solution.py:281
  214.8 30.5 %collective-permute-start.16 = (bf16[2,128,1024]{2,1,0:T(8,128)(2,1)S(1)}, bf16[2,128,1024]{2,1,0:T(8,128)(2,1)S(1)}, u32[]{:S(2)}, u32[]{:S(2)}) collective-permute-start(bf16[2,128,1024]{2,1,0:T(8,128)(2,1)S(1)} %constant_dynamic-update-slice_fusion.10.refs_12_), channel_id=1, source_target_pairs={{0,4},{4,0},{8,12},{12,8},{16,20},{20,16},{24,28},{28,24},{1,5},{5... | collective-permute-start | bytes 1572872 | tf_op jit(solution)/shard_map/ppermute | solution.py:281
  215.3 30.0 %collective-permute-start.12 = (bf16[2,128,1024]{2,1,0:T(8,128)(2,1)S(1)}, bf16[2,128,1024]{2,1,0:T(8,128)(2,1)S(1)}, u32[]{:S(2)}, u32[]{:S(2)}) collective-permute-start(bf16[2,128,1024]{2,1,0:T(8,128)(2,1)S(1)} %constant_dynamic-update-slice_fusion.8.refs_8_), channel_id=1, source_target_pairs={{0,4},{4,0},{8,12},{12,8},{16,20},{20,16},{24,28},{28,24},{1,5},{5... | collective-permute-start | bytes 1572872 | tf_op jit(solution)/shard_map/ppermute | solution.py:281
  226.8 18.5 %collective-permute-start.17 = (bf16[2,128,1024]{2,1,0:T(8,128)(2,1)S(1)}, bf16[2,128,1024]{2,1,0:T(8,128)(2,1)}, u32[]{:S(2)}, u32[]{:S(2)}) collective-permute-start(bf16[2,128,1024]{2,1,0:T(8,128)(2,1)S(1)} %collective-permute-done.15.refs_13_), channel_id=1, source_target_pairs={{0,4},{4,0},{8,12},{12,8},{16,20},{20,16},{24,28},{28,24},{1,5},{5... | collective-permute-start | bytes 1572872 | tf_op jit(solution)/shard_map/ppermute | solution.py:281
  226.8 18.5 %collective-permute-start.13 = (bf16[2,128,1024]{2,1,0:T(8,128)(2,1)S(1)}, bf16[2,128,1024]{2,1,0:T(8,128)(2,1)}, u32[]{:S(2)}, u32[]{:S(2)}) collective-permute-start(bf16[2,128,1024]{2,1,0:T(8,128)(2,1)S(1)} %collective-permute-done.11.refs_9_), channel_id=1, source_target_pairs={{0,4},{4,0},{8,12},{12,8},{16,20},{20,16},{24,28},{28,24},{1,5},{5... | collective-permute-start | bytes 1572872 | tf_op jit(solution)/shard_map/ppermute | solution.py:281
  (42 other events, 821.6 us)
